TPU v7x, 256 devices: a whole 4x4x8 slice. The times are simulated.
256 devices in a mesh: shard: 64 (over y, z_lo, x, core), tensor: 4 (over z_hi).
Axes of the slice: x: 4, y: 4, z: 8 (z_hi: 4, z_lo: 2; z = z_hi * 2 + z_lo), core: 2. Of those that a mesh axis runs over, the one named last changes fastest.
Arguments:
- grads: bfloat16 [256, 1024, 1024], P(None, 'shard', 'tensor'), may hold values from -48 to 48
- momentum: float32 [256, 1024, 1024], P(None, 'shard', 'tensor'), may hold values from -6 to 6
Outputs:
- momentum_next: float32 [256, 1024, 1024], P(None, 'shard', 'tensor')
- update: bfloat16 [256, 1024, 1024], P(None, 'shard', 'tensor')
All inputs are finite; a program needn't handle non-finite values.
Results may differ from a plain program's by a relative error of at most 0.012.
Values may be sent and summed in bfloat16 or wider, within the bound.
A program may use at most 64 MiB of HBM per device.

v0:
```python
import jax
import jax.numpy as jnp
from jax import lax
from jax.sharding import PartitionSpec as P

NS_STEPS = 2


def orthogonalize(whole, norm_value):
    current = (whole.astype(jnp.float32) / (norm_value + 1e-07)).astype(jnp.bfloat16)
    for step in range(NS_STEPS):
        gram = lax.dot_general(
            current, current, (((1,), (1,)), ((), ())), preferred_element_type=jnp.float32
        ).astype(jnp.bfloat16)
        power_f = jnp.dot(gram, current, preferred_element_type=jnp.float32)
        power = power_f.astype(jnp.bfloat16)
        square = jnp.dot(gram, power, preferred_element_type=jnp.float32)
        current = (3.4445 * current.astype(jnp.float32) - 4.775 * power_f + 2.0315 * square).astype(
            jnp.bfloat16
        )
    scale = 0.2 * float(whole.shape[0]) ** 0.5
    return (scale * current.astype(jnp.float32)).astype(jnp.bfloat16)


def shards(grads, momentum):
    grads_f = grads.astype(jnp.float32)
    momentum_next = 0.95 * momentum + grads_f
    nesterov = (grads_f + 0.95 * momentum_next).astype(jnp.bfloat16)
    count = nesterov.shape[0]
    row_part = nesterov.shape[1]
    col_part = nesterov.shape[2]
    shard_count = lax.axis_size("shard")
    tensor_count = lax.axis_size("tensor")
    sending = (
        nesterov.reshape(shard_count, tensor_count, row_part, col_part)
        .transpose(1, 0, 2, 3)
        .reshape(count, row_part, col_part)
    )
    first = lax.all_to_all(sending, "tensor", split_axis=0, concat_axis=2, tiled=True)
    whole = lax.all_to_all(first, "shard", split_axis=0, concat_axis=1, tiled=True)
    block = whole[0]
    block_f = block.astype(jnp.float32)
    norm_value = jnp.sqrt(jnp.sum(block_f * block_f))
    result = orthogonalize(block, norm_value)[None]
    back_rows = lax.all_to_all(result, "shard", split_axis=1, concat_axis=0, tiled=True)
    back = lax.all_to_all(back_rows, "tensor", split_axis=2, concat_axis=0, tiled=True)
    update = (
        back.reshape(tensor_count, shard_count, row_part, col_part)
        .transpose(1, 0, 2, 3)
        .reshape(count, row_part, col_part)
    )
    return (momentum_next, update)


def solution(mesh):
    return jax.shard_map(
        shards,
        mesh=mesh,
        in_specs=(P(None, "shard", "tensor"), P(None, "shard", "tensor")),
        out_specs=(P(None, "shard", "tensor"), P(None, "shard", "tensor")),
        check_vma=False,
    )
```

profile of v0, /device:TPU:1, one launch (start us, length us, event | category | flops | bytes accessed | tf_op | source)
XLA Modules:
  0.0 271.9 jit_solution(2860784223506038048)
XLA Ops:
  0.6 5.7 %fusion = (bf16[256,16,256]{2,1,0:T(8,128)(2,1)S(1)}, f32[256,16,256]{2,1,0:T(8,128)}) fusion(bf16[256,16,256]{2,1,0:T(8,128)(2,1)} %param.2, f32[256,16,256]{2,1,0:T(8,128)} %param.3), kind=kLoop, calls=%fused_computation.4 | loop fusion | flops 6291456 | bytes 12582912 | tf_op jit(solution)/shard_map/convert_element_type | solution.py:28
  6.4 0.2 copy.19
  6.6 56.6 %all_to_all.48 = bf16[256,16,256]{2,1,0:T(8,128)(2,1)S(1)} all-to-all(bf16[256,16,256]{2,1,0:T(8,128)(2,1)S(1)} %bitcast.35), channel_id=1, replica_groups=mesh['shard'=64,'tensor'=4] {'tensor'}, dimensions={0} | all-to-all | bytes 4194304 | tf_op jit(solution)/shard_map/all_to_all | solution.py:39
  63.2 0.3 copy.32
  63.5 40.2 %all_to_all.49 = bf16[64,16,1024]{2,1,0:T(8,128)(2,1)S(1)} all-to-all(bf16[64,16,1024]{2,1,0:T(8,128)(2,1)S(1)} %bitcast.37), channel_id=1, replica_groups=mesh['shard'=64,'tensor'=4] {'shard'}, dimensions={0} | all-to-all | bytes 4194304 | tf_op jit(solution)/shard_map/all_to_all | solution.py:40
  103.7 1.7 fusion.1
  106.1 0.5 fusion.2
  106.6 2.4 convolution_convert_fusion.1
  109.0 2.3 fusion.9
  111.3 2.6 add_convert_fusion.1
  114.0 2.4 convolution_convert_fusion
  116.3 2.3 fusion.10
  118.7 3.0 %fusion.3 = bf16[1,1024,1024]{2,1,0:T(8,128)(2,1)S(1)} fusion(bf16[1024,1024]{1,0:T(8,128)(2,1)S(1)} %convolution_convert_fusion, f32[1024,1024]{1,0:T(8,128)S(1)} %fusion.10, bf16[1024,1024]{1,0:T(8,128)(2,1)S(1)} %add_convert_fusion.1), kind=kOutput, calls=%fused_computation.10 | convolution fusion | flops 2159017984 | bytes 10485760 | tf_op jit(solution)/shard_map/dot_general | solution.py:17
  121.7 5.2 %copy.34 = bf16[1,1024,1024]{2,0,1:T(2,128)(2,1)} copy(bf16[1,1024,1024]{2,1,0:T(8,128)(2,1)S(1)} %fusion.3) | data formatting | bytes 4194304 | tf_op jit(solution)/shard_map/broadcast_in_dim | solution.py:44
  126.8 0.5 broadcast.36
  127.3 12.8 %reduce.3 = bf16[1024,1024]{1,0:T(8,128)(2,1)S(1)} reduce(bf16[1024,1,1024]{2,1,0:T(2,128)(2,1)} %bitcast.30, bf16[]{:T(256)} %broadcast.36), dimensions={1}, to_apply=%bitcast.29.reduce_sub_computation | reduce | bytes 4194306
  140.1 2.8 %reshape.37 = bf16[64,2,8192]{2,1,0:T(2,128)(2,1)} reshape(bf16[1024,1024]{1,0:T(8,128)(2,1)S(1)} %reduce.3) | data formatting | bytes 4194304
  142.9 33.8 %all_to_all.50 = bf16[64,2,8192]{2,1,0:T(2,128)(2,1)S(1)} all-to-all(bf16[64,2,8192]{2,1,0:T(2,128)(2,1)} %reshape.37), channel_id=1, replica_groups=mesh['shard'=64,'tensor'=4] {'shard'}, dimensions={0} | all-to-all | bytes 4194304 | tf_op jit(solution)/shard_map/all_to_all | solution.py:45
  176.6 6.8 %reshape.38 = bf16[1024,1,1024]{2,1,0:T(2,128)(2,1)} reshape(bf16[64,2,8192]{2,1,0:T(2,128)(2,1)S(1)} %all_to_all.50) | data formatting | bytes 4194304
  183.4 3.0 %copy.27 = bf16[1,1024,1024]{2,1,0:T(8,128)(2,1)S(1)} copy(bf16[1,1024,1024]{2,0,1:T(2,128)(2,1)} %bitcast.31) | data formatting | bytes 4194304
  186.4 6.1 %copy.22 = bf16[64,16,1024]{0,1,2:T(8,128)(2,1)} copy(bf16[64,16,1024]{2,1,0:T(8,128)(2,1)S(1)} %bitcast.34) | data formatting | bytes 4194304 | tf_op jit(solution)/shard_map/all_to_all | solution.py:45
  192.5 4.9 %reshape.39 = bf16[4,2,131072]{2,1,0:T(2,128)(2,1)S(1)} reshape(bf16[1024,16,64]{2,1,0:T(8,128)(2,1)} %bitcast.32) | data formatting | bytes 4194304
  197.5 53.0 %all_to_all.51 = bf16[4,2,131072]{2,1,0:T(2,128)(2,1)} all-to-all(bf16[4,2,131072]{2,1,0:T(2,128)(2,1)S(1)} %reshape.39), channel_id=1, replica_groups=mesh['shard'=64,'tensor'=4] {'tensor'}, dimensions={0} | all-to-all | bytes 4194304 | tf_op jit(solution)/shard_map/all_to_all | solution.py:46
  250.5 5.8 %reshape.40 = bf16[1024,16,64]{2,1,0:T(8,128)(2,1)} reshape(bf16[4,2,131072]{2,1,0:T(2,128)(2,1)} %all_to_all.51) | data formatting | bytes 4194304
  256.3 3.9 %fusion.8 = (bf16[64,16,256]{0,1,2:T(8,128)(2,1)S(1)}, bf16[64,16,256]{0,1,2:T(8,128)(2,1)S(1)}, bf16[64,16,256]{0,1,2:T(8,128)(2,1)S(1)}, bf16[64,16,256]{0,1,2:T(8,128)(2,1)}) fusion(bf16[64,16,1024]{0,1,2:T(8,128)(2,1)} %bitcast.33), kind=kLoop, calls=%fused_computation.16 | loop fusion | bytes 4194304 | tf_op jit(solution)/shard_map/slice
  260.1 3.4 %copy.31 = bf16[64,16,256]{2,1,0:T(8,128)(2,1)} copy(bf16[64,16,256]{0,1,2:T(8,128)(2,1)} %get-tuple-element.9) | data formatting | bytes 1048576
  263.5 2.2 copy.30
  265.7 0.0 copy-start
  265.7 0.0 copy-start.1
  265.7 2.2 copy.29
  267.9 1.3 copy.28
  269.2 0.0 copy-done
  269.2 0.0 copy-done.1
  269.2 2.6 pad_maximum_fusion
Async XLA Ops:
  265.7 3.5 %copy-start = (bf16[64,16,256]{2,1,0:T(8,128)(2,1)S(1)}, bf16[64,16,256]{2,1,0:T(8,128)(2,1)}, u32[]{:S(2)}) copy-start(bf16[64,16,256]{2,1,0:T(8,128)(2,1)} %copy.31) | copy-start | bytes 1572868
  265.7 3.5 %copy-start.1 = (bf16[64,16,256]{2,1,0:T(8,128)(2,1)S(1)}, bf16[64,16,256]{2,1,0:T(8,128)(2,1)}, u32[]{:S(2)}) copy-start(bf16[64,16,256]{2,1,0:T(8,128)(2,1)} %copy.30) | copy-start | bytes 1572868
where the time goes:
time: 272 us
  blocking collectives  184 us (68%)
  local copies, waits for them, and re-layouts  48.5 us (18%)
  other arithmetic  23.3 us (9%)
  matrix products  15 us (6%)
    all_to_all x1, blocking collectives, shards(): lax.all_to_all(sending, 'tensor', split_axis=0, concat_axis=2, tiled=True)  56.6 us
    all_to_all x1, blocking collectives, shards(): lax.all_to_all(back_rows, 'tensor', split_axis=2, concat_axis=0, tiled=True)  53 us
    all_to_all x1, blocking collectives, shards(): lax.all_to_all(first, 'shard', split_axis=0, concat_axis=1, tiled=True)  40.2 us
    all_to_all x1, blocking collectives, shards(): lax.all_to_all(result, 'shard', split_axis=1, concat_axis=0, tiled=True)  33.8 us
    unnamed x14, local copies, waits for them, and re-layouts  32.9 us
    unnamed x1, other arithmetic  12.8 us
    all_to_all x1, local copies, waits for them, and re-layouts, shards(): lax.all_to_all(result, 'shard', split_axis=1, concat_axis=0, tiled=True)  6.13 us
    convert_element_type x1, other arithmetic, shards(): nesterov = (grads_f + 0.95 * momentum_next).astype(jnp.bfloat16)  5.75 us

commit v1 on v0

v1 whole, which is shorter than its diff:
```python
import functools

import jax
import jax.numpy as jnp
from jax import lax
from jax.experimental import pallas as pl
from jax.experimental.pallas import tpu as pltpu
from jax.sharding import PartitionSpec as P

MESH = pl.DeviceIdType.MESH
NT = (((1,), (1,)), ((), ()))
A, B, C = 3.4445, -4.775, 2.0315
HOPS = (4, 1, -1, 2, -2, 3, -3, 0)


def place():
    shard = lax.axis_index("shard")
    tensor = lax.axis_index("tensor")
    return (shard // 2) % 4, shard // 16, tensor * 2 + (shard // 8) % 2, shard % 2


def mesh_index(x, y, z, core):
    return y * 16 + (z % 2) * 8 + x * 2 + core, z // 2


def dot(left, right, dims=(((1,), (0,)), ((), ()))):
    return lax.dot_general(left, right, dims, preferred_element_type=jnp.float32)


def kernel(nest, out, whole, gram_f, gram, poly, mid, upd, send_sem, recv_sem, back_send_sem, back_recv_sem):
    my_shard, my_tensor = lax.axis_index("shard"), lax.axis_index("tensor")
    me = my_shard * 4 + my_tensor
    x, y, z, core = place()

    barrier = pltpu.get_barrier_semaphore()

    def greet(step, carry):
        to = (lax.rem(my_shard + step // 4, 64), lax.rem(my_tensor + step % 4, 4))
        pl.semaphore_signal(barrier, inc=1, device_id=to, device_id_type=MESH)
        return carry

    lax.fori_loop(1, 256, greet, 0)
    pl.semaphore_wait(barrier, 255)

    own = pltpu.make_async_copy(nest.at[me], whole.at[my_tensor, my_shard], recv_sem)
    own.start()

    def forward(to_x, to_y, to_z, to_core):
        shard, tensor = mesh_index(to_x, to_y, to_z, to_core)
        pltpu.make_async_remote_copy(
            src_ref=nest.at[shard * 4 + tensor],
            dst_ref=whole.at[my_tensor, my_shard],
            send_sem=send_sem,
            recv_sem=recv_sem,
            device_id=(shard, tensor),
            device_id_type=MESH,
        ).start()

    for to_core in (0, 1):

        def to_plane(step, carry, to_core=to_core):
            to_x, to_y = (x + step) % 4, (y + step // 4) % 4
            for hop in HOPS:
                if hop == 0:

                    @pl.when((step > 0) | (core != to_core))
                    def _():
                        forward(to_x, to_y, z, to_core)
                else:
                    forward(to_x, to_y, (z + hop) % 8, to_core)
            return carry

        lax.fori_loop(0, 16, to_plane, 0)

    pltpu.make_async_copy(whole, whole, recv_sem).wait()

    def panel(ref, t, i):
        return ref[t, pl.ds(i * 16, 16)].reshape(256, 256)

    def make_gram(ref, i):
        total = None
        for t in range(4):
            part = dot(panel(ref, t, i), ref[t].reshape(1024, 256), NT)
            total = part if total is None else total + part
        return total

    def rows(i):
        return pl.ds(pl.multiple_of(i * 256, 256), 256)

    def first_gram(i, carry):
        gram_f[rows(i), :] = make_gram(whole, i)
        return carry

    lax.fori_loop(0, 4, first_gram, 0)
    squares = jnp.zeros((256, 256), jnp.float32)
    diagonal = lax.broadcasted_iota(jnp.int32, (256, 256), 0) == lax.broadcasted_iota(jnp.int32, (256, 256), 1)
    for i in range(4):
        squares += jnp.where(diagonal, gram_f[256 * i : 256 * i + 256, 256 * i : 256 * i + 256], 0.0)
    norm = jnp.sqrt(jnp.sum(squares, keepdims=True))
    scale = 1.0 / (norm + 1e-7)

    def round_gram(i, carry):
        gram[rows(i), :] = (gram_f[rows(i), :] * (scale * scale)).astype(jnp.bfloat16)
        return carry

    lax.fori_loop(0, 4, round_gram, 0)

    def make_poly(i, carry):
        strip = gram[rows(i), :]
        poly[rows(i), :] = (B * strip.astype(jnp.float32) + C * dot(strip, gram[...])).astype(jnp.bfloat16)
        return carry

    lax.fori_loop(0, 4, make_poly, 0)

    def first_step(i, carry):
        for t in range(4):
            value = A * panel(whole, t, i).astype(jnp.float32) + dot(poly[rows(i), :], whole[t].reshape(1024, 256))
            mid[t, pl.ds(i * 16, 16)] = (value * scale).astype(jnp.bfloat16).reshape(16, 16, 256)
        return carry

    lax.fori_loop(0, 4, first_step, 0)

    def second_gram(i, carry):
        gram[rows(i), :] = make_gram(mid, i).astype(jnp.bfloat16)
        return carry

    lax.fori_loop(0, 4, second_gram, 0)
    lax.fori_loop(0, 4, make_poly, 0)

    def backward(to_x, to_y, to_z, to_core):
        shard, tensor = mesh_index(to_x, to_y, to_z, to_core)
        pltpu.make_async_remote_copy(
            src_ref=upd.at[tensor, shard],
            dst_ref=out.at[me],
            send_sem=back_send_sem,
            recv_sem=back_recv_sem,
            device_id=(shard, tensor),
            device_id_type=MESH,
        ).start()

    def second_step(step, carry):
        to_y = (y + step) % 4
        for t in range(4):
            value = A * panel(mid, t, to_y).astype(jnp.float32) + dot(poly[rows(to_y), :], mid[t].reshape(1024, 256))
            upd[t, pl.ds(to_y * 16, 16)] = (0.2 * 32.0 * value).astype(jnp.bfloat16).reshape(16, 16, 256)

        def to_line(line, carry):
            to_x, to_core = (x + line // 2) % 4, (core + line) % 2
            for hop in HOPS:
                if hop == 0:

                    @pl.when((step > 0) | (line > 0))
                    def _():
                        backward(to_x, to_y, z, to_core)
                else:
                    backward(to_x, to_y, (z + hop) % 8, to_core)
            return carry

        lax.fori_loop(0, 8, to_line, 0)
        return carry

    lax.fori_loop(0, 4, second_step, 0)
    kept = pltpu.make_async_copy(upd.at[my_tensor, my_shard], out.at[me], back_recv_sem)
    kept.start()

    sent = nest.at[pl.ds(0, 255)]
    pltpu.make_async_copy(sent, sent, send_sem).wait()
    pltpu.make_async_copy(sent, sent, back_send_sem).wait()
    pltpu.make_async_copy(out, out, back_recv_sem).wait()


def shards(grads, momentum):
    grads_f = grads.astype(jnp.float32)
    momentum_next = 0.95 * momentum + grads_f
    nesterov = (grads_f + 0.95 * momentum_next).astype(jnp.bfloat16)
    vmem = pl.BlockSpec(memory_space=pltpu.VMEM)
    panels = (4, 64, 16, 256)
    update = pl.pallas_call(
        kernel,
        name="muon",
        out_shape=jax.ShapeDtypeStruct(nesterov.shape, jnp.bfloat16),
        in_specs=[vmem],
        out_specs=vmem,
        scratch_shapes=[
            pltpu.VMEM(panels, jnp.bfloat16),
            pltpu.VMEM((1024, 1024), jnp.float32),
            pltpu.VMEM((1024, 1024), jnp.bfloat16),
            pltpu.VMEM((1024, 1024), jnp.bfloat16),
            pltpu.VMEM(panels, jnp.bfloat16),
            pltpu.VMEM(panels, jnp.bfloat16),
            pltpu.SemaphoreType.DMA,
            pltpu.SemaphoreType.DMA,
            pltpu.SemaphoreType.DMA,
            pltpu.SemaphoreType.DMA,
        ],
        compiler_params=pltpu.CompilerParams(collective_id=0, has_side_effects=True),
    )(nesterov)
    return (momentum_next, update)


def solution(mesh):
    spec = P(None, "shard", "tensor")
    return jax.shard_map(shards, mesh=mesh, in_specs=(spec, spec), out_specs=(spec, spec), check_vma=False)
```

time: 272 us -> 122 us (0.45)
  blocking collectives: 184 us -> 0 us
  Pallas kernels: 0 us -> 112 us
  local copies, waits for them, and re-layouts: 48.5 us -> 3.05 us
  other arithmetic: 23.3 us -> 6.38 us
  matrix products: 15 us -> 0 us
    all_to_all x4 -> x0, blocking collectives: 184 us -> none  [the longest x1 56.6 us: shards(): lax.all_to_all(sending, 'tensor', split_axis=0, concat_axis=2, tiled=True)]
    pallas_call x0 -> x1, Pallas kernels: none -> 112 us  [shards(): pl.pallas_call(kernel, name='muon', out_shape=jax.ShapeDtypeStruct(nester...]
    unnamed x14 -> x1, local copies, waits for them, and re-layouts: 32.9 us -> 3.05 us
    dot_general x6 -> x0, matrix products: 15 us -> none  [the longest x2 5.61 us: orthogonalize(): square = jnp.dot(gram, power, preferred_element_type=jnp.float32)]
    unnamed x1 -> x0, other arithmetic: 12.8 us -> none
    all_to_all x2 -> x0, local copies, waits for them, and re-layouts: 6.4 us -> none  [the longest x1 6.13 us: shards(): lax.all_to_all(result, 'shard', split_axis=1, concat_axis=0, tiled=True)]
    broadcast_in_dim x1 -> x0, local copies, waits for them, and re-layouts: 5.16 us -> none  [shards(): result = orthogonalize(block, norm_value)[None]]
    slice x1 -> x0, local copies, waits for them, and re-layouts: 3.86 us -> none
where the time goes in v1:
time: 122 us
  Pallas kernels  112 us (92%)
  other arithmetic  6.38 us (5%)
  local copies, waits for them, and re-layouts  3.05 us (2%)
    pallas_call x1, Pallas kernels, shards(): pl.pallas_call(kernel, name='muon', out_shape=jax.ShapeDtypeStruct(nester...  112 us
    convert_element_type x1, other arithmetic, shards(): nesterov = (grads_f + 0.95 * momentum_next).astype(jnp.bfloat16)  6.38 us
    unnamed x1, local copies, waits for them, and re-layouts  3.05 us

profile of v1, /device:TPU:1, one launch (start us, length us, event | category | flops | bytes accessed | tf_op | source)
XLA Modules:
  0.0 122.1 jit_solution(9090166620072444664)
XLA Ops:
  0.6 6.4 %fusion = (bf16[256,16,256]{2,1,0:T(8,128)(2,1)}, f32[256,16,256]{2,1,0:T(8,128)}) fusion(bf16[256,16,256]{2,1,0:T(8,128)(2,1)} %param.2, f32[256,16,256]{2,1,0:T(8,128)} %param.3), kind=kLoop, calls=%fused_computation.2 | loop fusion | flops 6291456 | bytes 12582912 | tf_op jit(solution)/shard_map/convert_element_type | solution.py:175
  7.0 112.0 %muon.1 = bf16[256,16,256]{2,1,0:T(8,128)(2,1)} custom-call(bf16[256,16,256]{2,1,0:T(8,128)(2,1)} %get-tuple-element.2.nest), custom_call_target="tpu_custom_call" | custom-call | tf_op jit(solution)/shard_map/muon/pallas_call | solution.py:178
  119.0 3.0 %copy.5 = bf16[256,16,256]{2,1,0:T(8,128)(2,1)} copy(bf16[256,16,256]{2,1,0:T(8,128)(2,1)} %muon.1) | data formatting | bytes 4194304

commit v2 on v1

--- a/solution.py
+++ b/solution.py
@@ -1,5 +1,3 @@
-import functools
-
 import jax
 import jax.numpy as jnp
 from jax import lax
@@ -10,6 +8,7 @@
 MESH = pl.DeviceIdType.MESH
 NT = (((1,), (1,)), ((), ()))
 A, B, C = 3.4445, -4.775, 2.0315
+CHUNK = 32
 HOPS = (4, 1, -1, 2, -2, 3, -3, 0)
 
 
@@ -27,19 +26,50 @@
     return lax.dot_general(left, right, dims, preferred_element_type=jnp.float32)
 
 
-def kernel(nest, out, whole, gram_f, gram, poly, mid, upd, send_sem, recv_sem, back_send_sem, back_recv_sem):
+def kernel(grads, momentum, kept, out, fresh, nest, whole, gram_f, gram, poly, mid, upd, load_sem, send_sem, recv_sem, back_send_sem, back_recv_sem):
     my_shard, my_tensor = lax.axis_index("shard"), lax.axis_index("tensor")
     me = my_shard * 4 + my_tensor
     x, y, z, core = place()
 
+    def load(i):
+        part = pl.ds(i * CHUNK, CHUNK)
+        return (
+            pltpu.make_async_copy(grads.at[part], fresh.at[part], load_sem.at[0, i]),
+            pltpu.make_async_copy(momentum.at[part], kept.at[part], load_sem.at[1, i]),
+        )
+
+    for i in range(256 // CHUNK):
+        for copy in load(i):
+            copy.start()
+
     barrier = pltpu.get_barrier_semaphore()
+    depths = [(z + hop) % 8 for hop in (4, 3, 5, 2, 6, 1, 7, 0)]
+    depths = [((depth % 2) * 8, depth // 2) for depth in depths]
 
     def greet(step, carry):
-        to = (lax.rem(my_shard + step // 4, 64), lax.rem(my_tensor + step % 4, 4))
-        pl.semaphore_signal(barrier, inc=1, device_id=to, device_id_type=MESH)
-        return carry
-
-    lax.fori_loop(1, 256, greet, 0)
+        column = ((y + 2 + step // 4) % 4) * 16 + ((x + 2 + step) % 4) * 2
+        for low, tensor in depths:
+            for other in (0, 1):
+                shard = column + low + other
+
+                @pl.when((shard != my_shard) | (tensor != my_tensor))
+                def _():
+                    pl.semaphore_signal(barrier, inc=1, device_id=(shard, tensor), device_id_type=MESH)
+        return carry
+
+    lax.fori_loop(0, 16, greet, 0)
+
+    def blend(i, carry):
+        for copy in load(i):
+            copy.wait()
+        part = pl.ds(i * CHUNK, CHUNK)
+        grads_f = fresh[part].astype(jnp.float32)
+        momentum_next = 0.95 * kept[part] + grads_f
+        kept[part] = momentum_next
+        nest[part] = (grads_f + 0.95 * momentum_next).astype(jnp.bfloat16)
+        return carry
+
+    lax.fori_loop(0, 256 // CHUNK, blend, 0)
     pl.semaphore_wait(barrier, 255)
 
     own = pltpu.make_async_copy(nest.at[me], whole.at[my_tensor, my_shard], recv_sem)
@@ -160,8 +190,8 @@
         return carry
 
     lax.fori_loop(0, 4, second_step, 0)
-    kept = pltpu.make_async_copy(upd.at[my_tensor, my_shard], out.at[me], back_recv_sem)
-    kept.start()
+    stay = pltpu.make_async_copy(upd.at[my_tensor, my_shard], out.at[me], back_recv_sem)
+    stay.start()
 
     sent = nest.at[pl.ds(0, 255)]
     pltpu.make_async_copy(sent, sent, send_sem).wait()
@@ -169,33 +199,54 @@
     pltpu.make_async_copy(out, out, back_recv_sem).wait()
 
 
+def write_out(kept, out, kept_hbm, out_hbm, sem):
+    copies = [pltpu.make_async_copy(kept, kept_hbm, sem.at[0]), pltpu.make_async_copy(out, out_hbm, sem.at[1])]
+    for copy in copies:
+        copy.start()
+    for copy in copies:
+        copy.wait()
+
+
 def shards(grads, momentum):
-    grads_f = grads.astype(jnp.float32)
-    momentum_next = 0.95 * momentum + grads_f
-    nesterov = (grads_f + 0.95 * momentum_next).astype(jnp.bfloat16)
     vmem = pl.BlockSpec(memory_space=pltpu.VMEM)
+    hbm = pl.BlockSpec(memory_space=pltpu.HBM)
     panels = (4, 64, 16, 256)
-    update = pl.pallas_call(
+    square = (1024, 1024)
+    kept, update = pl.pallas_call(
         kernel,
         name="muon",
-        out_shape=jax.ShapeDtypeStruct(nesterov.shape, jnp.bfloat16),
-        in_specs=[vmem],
-        out_specs=vmem,
+        out_shape=(pltpu.VMEM(momentum.shape, jnp.float32), pltpu.VMEM(grads.shape, jnp.bfloat16)),
+        in_specs=[hbm, hbm],
+        out_specs=(vmem, vmem),
         scratch_shapes=[
+            pltpu.VMEM(grads.shape, jnp.bfloat16),
+            pltpu.VMEM(grads.shape, jnp.bfloat16),
             pltpu.VMEM(panels, jnp.bfloat16),
-            pltpu.VMEM((1024, 1024), jnp.float32),
-            pltpu.VMEM((1024, 1024), jnp.bfloat16),
-            pltpu.VMEM((1024, 1024), jnp.bfloat16),
+            pltpu.VMEM(square, jnp.float32),
+            pltpu.VMEM(square, jnp.bfloat16),
+            pltpu.VMEM(square, jnp.bfloat16),
             pltpu.VMEM(panels, jnp.bfloat16),
             pltpu.VMEM(panels, jnp.bfloat16),
+            pltpu.SemaphoreType.DMA((2, 256 // CHUNK)),
             pltpu.SemaphoreType.DMA,
             pltpu.SemaphoreType.DMA,
             pltpu.SemaphoreType.DMA,
             pltpu.SemaphoreType.DMA,
         ],
-        compiler_params=pltpu.CompilerParams(collective_id=0, has_side_effects=True),
-    )(nesterov)
-    return (momentum_next, update)
+        compiler_params=pltpu.CompilerParams(collective_id=0, has_side_effects=True, vmem_limit_bytes=57 * 2**20),
+    )(grads, momentum)
+    return pl.pallas_call(
+        write_out,
+        name="write_out",
+        out_shape=(
+            jax.ShapeDtypeStruct(momentum.shape, jnp.float32),
+            jax.ShapeDtypeStruct(grads.shape, jnp.bfloat16),
+        ),
+        in_specs=[vmem, vmem],
+        out_specs=(hbm, hbm),
+        scratch_shapes=[pltpu.SemaphoreType.DMA((2,))],
+        compiler_params=pltpu.CompilerParams(vmem_limit_bytes=2**20),
+    )(kept, update)
 
 
 def solution(mesh):

time: 122 us -> 111 us (0.910)
  other arithmetic: 6.38 us -> 0 us
  local copies, waits for them, and re-layouts: 3.05 us -> 0 us
  Pallas kernels: 112 us -> 110 us
    convert_element_type x1 -> x0, other arithmetic: 6.38 us -> none  [shards(): nesterov = (grads_f + 0.95 * momentum_next).astype(jnp.bfloat16)]
    unnamed x1 -> x0, local copies, waits for them, and re-layouts: 3.05 us -> none
    pallas_call x1 -> x2, Pallas kernels: 112 us -> 110 us  [the longest x1 107 us: shards(): pl.pallas_call(kernel, name='muon', out_shape=(pltpu.VMEM(momentum.shape,...]
where the time goes in v2:
time: 111 us; the launch traced here: 110 us
  Pallas kernels  110 us (99%)
    pallas_call x1, Pallas kernels, shards(): pl.pallas_call(kernel, name='muon', out_shape=(pltpu.VMEM(momentum.shape,...  107 us
    pallas_call x1, Pallas kernels, shards(): pl.pallas_call(write_out, name='write_out', out_shape=(jax.ShapeDtypeStru...  2.72 us

profile of v2, /device:TPU:1, one launch (start us, length us, event | category | flops | bytes accessed | tf_op | source)
XLA Modules:
  0.0 110.2 jit_solution(584987181696976362)
XLA Ops:
  0.6 106.8 %muon.1 = (f32[256,16,256]{2,1,0:T(8,128)S(1)}, bf16[256,16,256]{2,1,0:T(8,128)(2,1)S(1)}) custom-call(bf16[256,16,256]{2,1,0:T(8,128)(2,1)} %grads.1, f32[256,16,256]{2,1,0:T(8,128)} %momentum.1), custom_call_target="tpu_custom_call" | custom-call | tf_op jit(solution)/shard_map/muon/pallas_call | solution.py:215
  107.4 2.7 %write_out.1 = (f32[256,16,256]{2,1,0:T(8,128)}, bf16[256,16,256]{2,1,0:T(8,128)(2,1)}) custom-call(f32[256,16,256]{2,1,0:T(8,128)S(1)} %get-tuple-element.4.kept, bf16[256,16,256]{2,1,0:T(8,128)(2,1)S(1)} %get-tuple-element.5.out), custom_call_target="tpu_custom_call" | custom-call | tf_op jit(solution)/shard_map/write_out/pallas_call | solution.py:238

commit v3 on v2

v3 whole, which is shorter than its diff:
```python
import jax
import jax.numpy as jnp
from jax import lax
from jax.experimental import pallas as pl
from jax.experimental.pallas import tpu as pltpu
from jax.sharding import PartitionSpec as P

MESH = pl.DeviceIdType.MESH
NN = (((1,), (0,)), ((), ()))
NT = (((1,), (1,)), ((), ()))
A, B, C = 3.4445, -4.775, 2.0315
EARLY = 5
HOPS = (4, 1, -1, 2, -2, 3, -3, 0)
BACK_HOPS = (4, 3, -3, 2, -2, 0, 1, -1)
OWNERS = (4, 2, 4, 2, 4)


def dot(left, right, dims=NN):
    return lax.dot_general(left, right, dims, preferred_element_type=jnp.float32)


def kernel(grads, momentum, kept, out, fresh, nest, whole, gram_f, gram, poly, mid, upd, load_sem, ready_sem, send_sem, recv_sem, back_send_sem, back_recv_sem):
    my_shard, my_tensor = lax.axis_index("shard"), lax.axis_index("tensor")
    x, y, core = (my_shard // 2) % 4, my_shard // 16, my_shard % 2
    my_low = (my_shard // 8) % 2
    z = my_tensor * 2 + my_low

    def depth(hop):
        to_z = (z + hop) % 8
        return to_z % 2, to_z // 2

    def shard_of(to_x, to_y, low, to_core):
        return to_y * 16 + low * 8 + to_x * 2 + to_core

    def column(step):
        return (x + step % 4) % 4, (y + step // 4) % 4

    def load(step):
        to_x, to_y = column(step)
        return (
            pltpu.make_async_copy(grads.at[to_y, :, to_x], fresh.at[to_y, :, to_x], load_sem.at[0, step]),
            pltpu.make_async_copy(momentum.at[to_y, :, to_x], kept.at[to_y, :, to_x], load_sem.at[1, step]),
        )

    def start_load(step, carry):
        for copy in load(step):
            copy.start()
        return carry

    lax.fori_loop(0, 2, start_load, 0)

    barrier = pltpu.get_barrier_semaphore()
    for hop in (4, 3, -3, 2, -2, 1, -1):
        low, tensor = depth(hop)
        for to_core in (0, 1):
            pl.semaphore_signal(barrier, inc=1, device_id=(shard_of(x, y, low, to_core), tensor), device_id_type=MESH)

    def greet(step, carry):
        to_x, to_y = column(step)
        for to_core in (0, 1):
            pl.semaphore_signal(barrier, inc=1, device_id=(shard_of(to_x, to_y, my_low, to_core), my_tensor), device_id_type=MESH)
        return carry

    lax.fori_loop(1, 16, greet, 0)
    pl.semaphore_signal(barrier, inc=1, device_id=(shard_of(x, y, my_low, 1 - core), my_tensor), device_id_type=MESH)
    lax.fori_loop(2, 16, start_load, 0)

    def blend(step, carry):
        for copy in load(step):
            copy.wait()
        to_x, to_y = column(step)
        for low in (0, 1):
            grads_f = fresh[to_y, low, to_x].astype(jnp.float32)
            momentum_next = 0.95 * kept[to_y, low, to_x] + grads_f
            kept[to_y, low, to_x] = momentum_next
            nest[to_y, low, to_x] = (grads_f + 0.95 * momentum_next).astype(jnp.bfloat16).reshape(2, 4, 16, 256)
        return carry

    def piece(ref, shard, tensor):
        return ref.at[shard, :, pl.ds(pl.multiple_of(tensor * 256, 256), 256)]

    def forward(to_x, to_y, hop, to_core):
        low, tensor = depth(hop)
        shard = shard_of(to_x, to_y, low, to_core)
        pltpu.make_async_remote_copy(
            src_ref=nest.at[to_y, low, to_x, to_core, tensor],
            dst_ref=piece(whole, my_shard, my_tensor),
            send_sem=send_sem,
            recv_sem=recv_sem,
            device_id=(shard, tensor),
            device_id_type=MESH,
        ).start()

    lax.fori_loop(0, 2, blend, 0)
    pl.semaphore_wait(barrier, 45)
    for hop in (4, 3, -3, 2, -2, 1, -1):
        low, tensor = depth(hop)
        pl.semaphore_signal(ready_sem, inc=1, device_id=(shard_of(x, y, low, core), tensor), device_id_type=MESH)

    for to_core in (0, 1):
        for hop in HOPS:
            if hop != 0:
                forward(x, y, hop, to_core)
    forward(x, y, 0, 1 - core)
    own = pltpu.make_async_copy(nest.at[y, my_low, x, core, my_tensor], piece(whole, my_shard, my_tensor), recv_sem)
    own.start()
    lax.fori_loop(2, EARLY + 1, blend, 0)
    pl.semaphore_wait(ready_sem, 7)

    def to_column(to_core, blending):
        def body(step, carry):
            to_x, to_y = column(step)
            for hop in HOPS:
                forward(to_x, to_y, hop, to_core)
            if blending:
                blend(step + EARLY, carry)
            return carry

        return body

    lax.fori_loop(1, 16 - EARLY, to_column(0, True), 0)
    lax.fori_loop(16 - EARLY, 16, to_column(0, False), 0)
    lax.fori_loop(1, 16, to_column(1, False), 0)
    pltpu.make_async_copy(whole, whole, recv_sem).wait()

    def rows(i):
        return pl.ds(pl.multiple_of(i * 256, 256), 256)

    def strip(ref, i):
        return ref[pl.ds(i * 16, 16)].reshape(256, 1024)

    def square(ref):
        return ref[...].reshape(1024, 1024)

    def first_gram(i, carry):
        gram_f[rows(i), :] = dot(strip(whole, i), square(whole), NT)
        return carry

    lax.fori_loop(0, 4, first_gram, 0)
    squares = jnp.zeros((256, 256), jnp.float32)
    diagonal = lax.broadcasted_iota(jnp.int32, (256, 256), 0) == lax.broadcasted_iota(jnp.int32, (256, 256), 1)
    for i in range(4):
        squares += jnp.where(diagonal, gram_f[256 * i : 256 * i + 256, 256 * i : 256 * i + 256], 0.0)
    norm = jnp.sqrt(jnp.sum(squares, keepdims=True))
    scale = 1.0 / (norm + 1e-7)

    def round_gram(i, carry):
        gram[rows(i), :] = (gram_f[rows(i), :] * (scale * scale)).astype(jnp.bfloat16)
        return carry

    lax.fori_loop(0, 4, round_gram, 0)

    def make_poly(i, carry):
        part = gram[rows(i), :]
        poly[rows(i), :] = (B * part.astype(jnp.float32) + C * dot(part, gram[...])).astype(jnp.bfloat16)
        return carry

    lax.fori_loop(0, 4, make_poly, 0)

    def first_step(i, carry):
        value = A * strip(whole, i).astype(jnp.float32) + dot(poly[rows(i), :], square(whole))
        mid[pl.ds(i * 16, 16)] = (value * scale).astype(jnp.bfloat16).reshape(16, 16, 1024)
        return carry

    lax.fori_loop(0, 4, first_step, 0)

    def second_gram(i, carry):
        gram[rows(i), :] = dot(strip(mid, i), square(mid), NT).astype(jnp.bfloat16)
        return carry

    lax.fori_loop(0, 4, second_gram, 0)
    lax.fori_loop(0, 4, make_poly, 0)

    def backward(to_x, to_y, hop, to_core):
        low, tensor = depth(hop)
        shard = shard_of(to_x, to_y, low, to_core)
        pltpu.make_async_remote_copy(
            src_ref=piece(upd, shard, tensor),
            dst_ref=out.at[y, my_low, x, core, my_tensor],
            send_sem=back_send_sem,
            recv_sem=back_recv_sem,
            device_id=(shard, tensor),
            device_id_type=MESH,
        ).start()

    def second_step(step, carry):
        to_y = (y + step) % 4
        value = A * strip(mid, to_y).astype(jnp.float32) + dot(poly[rows(to_y), :], square(mid))
        upd[pl.ds(to_y * 16, 16)] = (0.2 * 32.0 * value).astype(jnp.bfloat16).reshape(16, 16, 1024)
        return carry

    def send_strip(step):
        to_y = (y + step) % 4
        for hop in BACK_HOPS:

            def to_line(line, carry, hop=hop):
                to_x, to_core = (x + line // 2) % 4, (core + line) % 2
                if hop == 0:

                    @pl.when((step > 0) | (line > 0))
                    def _():
                        backward(to_x, to_y, hop, to_core)
                else:
                    backward(to_x, to_y, hop, to_core)
                return carry

            lax.fori_loop(0, 8, to_line, 0)

    def step_and_send(step, carry):
        second_step(step, carry)
        send_strip(step)
        return carry

    lax.fori_loop(0, 4, step_and_send, 0)
    stay = pltpu.make_async_copy(piece(upd, my_shard, my_tensor), out.at[y, my_low, x, core, my_tensor], back_recv_sem)
    stay.start()

    sent = whole.at[pl.ds(0, 63)]
    rest = piece(whole, 0, 0)
    for sem in (send_sem, back_send_sem):
        pltpu.make_async_copy(sent, sent, sem).wait()
        for _ in range(3):
            pltpu.make_async_copy(rest, rest, sem).wait()
    pltpu.make_async_copy(out, out, back_recv_sem).wait()


def write_out(kept, out, kept_hbm, out_hbm, sem):
    copies = [pltpu.make_async_copy(kept, kept_hbm, sem.at[0]), pltpu.make_async_copy(out, out_hbm, sem.at[1])]
    for copy in copies:
        copy.start()
    for copy in copies:
        copy.wait()


def shards(grads, momentum):
    vmem = pl.BlockSpec(memory_space=pltpu.VMEM)
    hbm = pl.BlockSpec(memory_space=pltpu.HBM)
    piece = grads.shape[1:]
    by_column = OWNERS[:3] + (8,) + piece
    by_owner = OWNERS + piece
    block = (64, 16, 1024)
    square = (1024, 1024)
    kept, update = pl.pallas_call(
        kernel,
        name="muon",
        out_shape=(pltpu.VMEM(by_column, jnp.float32), pltpu.VMEM(by_owner, jnp.bfloat16)),
        in_specs=[hbm, hbm],
        out_specs=(vmem, vmem),
        scratch_shapes=[
            pltpu.VMEM(by_column, jnp.bfloat16),
            pltpu.VMEM(by_owner, jnp.bfloat16),
            pltpu.VMEM(block, jnp.bfloat16),
            pltpu.VMEM(square, jnp.float32),
            pltpu.VMEM(square, jnp.bfloat16),
            pltpu.VMEM(square, jnp.bfloat16),
            pltpu.VMEM(block, jnp.bfloat16),
            pltpu.VMEM(block, jnp.bfloat16),
            pltpu.SemaphoreType.DMA((2, 16)),
            pltpu.SemaphoreType.REGULAR,
            pltpu.SemaphoreType.DMA,
            pltpu.SemaphoreType.DMA,
            pltpu.SemaphoreType.DMA,
            pltpu.SemaphoreType.DMA,
        ],
        compiler_params=pltpu.CompilerParams(collective_id=0, has_side_effects=True, vmem_limit_bytes=57 * 2**20),
    )(grads.reshape(by_column), momentum.reshape(by_column))
    return pl.pallas_call(
        write_out,
        name="write_out",
        out_shape=(
            jax.ShapeDtypeStruct(momentum.shape, jnp.float32),
            jax.ShapeDtypeStruct(grads.shape, jnp.bfloat16),
        ),
        in_specs=[vmem, vmem],
        out_specs=(hbm, hbm),
        scratch_shapes=[pltpu.SemaphoreType.DMA((2,))],
        compiler_params=pltpu.CompilerParams(vmem_limit_bytes=2**20),
    )(kept.reshape(momentum.shape), update.reshape(grads.shape))


def solution(mesh):
    spec = P(None, "shard", "tensor")
    return jax.shard_map(shards, mesh=mesh, in_specs=(spec, spec), out_specs=(spec, spec), check_vma=False)
```

time: 111 us -> 110 us (level)
  no operation moved by 1% of the time
where the time goes in v3:
time: 110 us
  Pallas kernels  109 us (99%)
    pallas_call x1, Pallas kernels, shards(): pl.pallas_call(kernel, name='muon', out_shape=(pltpu.VMEM(by_column, jnp....  106 us
    pallas_call x1, Pallas kernels, shards(): pl.pallas_call(write_out, name='write_out', out_shape=(jax.ShapeDtypeStru...  2.72 us

profile of v3, /device:TPU:1, one launch (start us, length us, event | category | flops | bytes accessed | tf_op | source)
XLA Modules:
  0.0 109.5 jit_solution(5552794871373295616)
XLA Ops:
  0.6 106.2 %muon.1 = (f32[4,2,4,8,16,256]{5,4,3,2,1,0:T(8,128)S(1)}, bf16[4,2,4,2,4,16,256]{6,5,4,3,2,1,0:T(8,128)(2,1)S(1)}) custom-call(bf16[4,2,4,8,16,256]{5,4,3,2,1,0:T(8,128)(2,1)} %bitcast.7, f32[4,2,4,8,16,256]{5,4,3,2,1,0:T(8,128)} %bitcast.6), custom_call_target="tpu_custom_call" | custom-call | tf_op jit(solution)/shard_map/muon/pallas_call | solution.py:243
  106.8 2.7 %write_out.1 = (f32[256,16,256]{2,1,0:T(8,128)}, bf16[256,16,256]{2,1,0:T(8,128)(2,1)}) custom-call(f32[256,16,256]{2,1,0:T(8,128)S(1)} %bitcast.4, bf16[256,16,256]{2,1,0:T(8,128)(2,1)S(1)} %bitcast.5), custom_call_target="tpu_custom_call" | custom-call | tf_op jit(solution)/shard_map/write_out/pallas_call | solution.py:267

commit v4 on v3

--- a/solution.py
+++ b/solution.py
@@ -11,7 +11,6 @@
 A, B, C = 3.4445, -4.775, 2.0315
 EARLY = 5
 HOPS = (4, 1, -1, 2, -2, 3, -3, 0)
-BACK_HOPS = (4, 3, -3, 2, -2, 0, 1, -1)
 OWNERS = (4, 2, 4, 2, 4)
 
 
@@ -19,7 +18,7 @@
     return lax.dot_general(left, right, dims, preferred_element_type=jnp.float32)
 
 
-def kernel(grads, momentum, kept, out, fresh, nest, whole, gram_f, gram, poly, mid, upd, load_sem, ready_sem, send_sem, recv_sem, back_send_sem, back_recv_sem):
+def kernel(grads, momentum, kept, out, fresh, nest, whole, gram, poly, mid, upd, load_sem, ready_sem, send_sem, recv_sem, back_send_sem, back_recv_sem):
     my_shard, my_tensor = lax.axis_index("shard"), lax.axis_index("tensor")
     x, y, core = (my_shard // 2) % 4, my_shard // 16, my_shard % 2
     my_low = (my_shard // 8) % 2
@@ -123,96 +122,80 @@
     lax.fori_loop(1, 16, to_column(1, False), 0)
     pltpu.make_async_copy(whole, whole, recv_sem).wait()
 
-    def rows(i):
-        return pl.ds(pl.multiple_of(i * 256, 256), 256)
+    def columns(j):
+        return pl.ds(pl.multiple_of(j * 256, 256), 256)
 
     def strip(ref, i):
         return ref[pl.ds(i * 16, 16)].reshape(256, 1024)
 
+    def panel(ref, j):
+        return ref[:, :, columns(j)].reshape(1024, 256)
+
     def square(ref):
         return ref[...].reshape(1024, 1024)
 
-    def first_gram(i, carry):
-        gram_f[rows(i), :] = dot(strip(whole, i), square(whole), NT)
-        return carry
-
-    lax.fori_loop(0, 4, first_gram, 0)
-    squares = jnp.zeros((256, 256), jnp.float32)
-    diagonal = lax.broadcasted_iota(jnp.int32, (256, 256), 0) == lax.broadcasted_iota(jnp.int32, (256, 256), 1)
-    for i in range(4):
-        squares += jnp.where(diagonal, gram_f[256 * i : 256 * i + 256, 256 * i : 256 * i + 256], 0.0)
-    norm = jnp.sqrt(jnp.sum(squares, keepdims=True))
-    scale = 1.0 / (norm + 1e-7)
-
-    def round_gram(i, carry):
-        gram[rows(i), :] = (gram_f[rows(i), :] * (scale * scale)).astype(jnp.bfloat16)
-        return carry
-
-    lax.fori_loop(0, 4, round_gram, 0)
-
-    def make_poly(i, carry):
-        part = gram[rows(i), :]
-        poly[rows(i), :] = (B * part.astype(jnp.float32) + C * dot(part, gram[...])).astype(jnp.bfloat16)
-        return carry
-
-    lax.fori_loop(0, 4, make_poly, 0)
-
-    def first_step(i, carry):
-        value = A * strip(whole, i).astype(jnp.float32) + dot(poly[rows(i), :], square(whole))
-        mid[pl.ds(i * 16, 16)] = (value * scale).astype(jnp.bfloat16).reshape(16, 16, 1024)
-        return carry
-
-    lax.fori_loop(0, 4, first_step, 0)
-
-    def second_gram(i, carry):
-        gram[rows(i), :] = dot(strip(mid, i), square(mid), NT).astype(jnp.bfloat16)
-        return carry
-
-    lax.fori_loop(0, 4, second_gram, 0)
-    lax.fori_loop(0, 4, make_poly, 0)
-
-    def backward(to_x, to_y, hop, to_core):
-        low, tensor = depth(hop)
-        shard = shard_of(to_x, to_y, low, to_core)
-        pltpu.make_async_remote_copy(
-            src_ref=piece(upd, shard, tensor),
-            dst_ref=out.at[y, my_low, x, core, my_tensor],
-            send_sem=back_send_sem,
-            recv_sem=back_recv_sem,
-            device_id=(shard, tensor),
-            device_id_type=MESH,
-        ).start()
-
-    def second_step(step, carry):
-        to_y = (y + step) % 4
-        value = A * strip(mid, to_y).astype(jnp.float32) + dot(poly[rows(to_y), :], square(mid))
-        upd[pl.ds(to_y * 16, 16)] = (0.2 * 32.0 * value).astype(jnp.bfloat16).reshape(16, 16, 1024)
-        return carry
-
-    def send_strip(step):
-        to_y = (y + step) % 4
-        for hop in BACK_HOPS:
-
-            def to_line(line, carry, hop=hop):
-                to_x, to_core = (x + line // 2) % 4, (core + line) % 2
-                if hop == 0:
-
-                    @pl.when((step > 0) | (line > 0))
-                    def _():
-                        backward(to_x, to_y, hop, to_core)
-                else:
-                    backward(to_x, to_y, hop, to_core)
-                return carry
-
-            lax.fori_loop(0, 8, to_line, 0)
+    def add_squares(i, total):
+        part = strip(whole, i).astype(jnp.float32)
+        return total + jnp.sum((part * part).reshape(32, 8, 1024), axis=0)
+
+    total = lax.fori_loop(0, 4, add_squares, jnp.zeros((8, 1024), jnp.float32))
+    scale = 1.0 / (jnp.sqrt(jnp.sum(total, keepdims=True)) + 1e-7)
+
+    def first_gram(j, carry):
+        gram[:, columns(j)] = (dot(square(whole), strip(whole, j), NT) * (scale * scale)).astype(jnp.bfloat16)
+        return carry
+
+    def make_poly(j, carry):
+        part = gram[:, columns(j)]
+        poly[:, columns(j)] = (B * part.astype(jnp.float32) + C * dot(gram[...], part)).astype(jnp.bfloat16)
+        return carry
+
+    def first_step(j, carry):
+        part = panel(whole, j)
+        value = A * part.astype(jnp.float32) + dot(poly[...], part)
+        mid[:, :, columns(j)] = (value * scale).astype(jnp.bfloat16).reshape(64, 16, 256)
+        return carry
+
+    def second_gram(j, carry):
+        gram[:, columns(j)] = dot(square(mid), strip(mid, j), NT).astype(jnp.bfloat16)
+        return carry
+
+    for body in (first_gram, make_poly, first_step, second_gram, make_poly):
+        lax.fori_loop(0, 4, body, 0)
+
+    def second_step(tensor):
+        part = panel(mid, tensor)
+        value = A * part.astype(jnp.float32) + dot(poly[...], part)
+        upd[tensor] = (0.2 * 32.0 * value).astype(jnp.bfloat16).reshape(64, 16, 256)
+
+    def send_panel(tensor):
+        def to_line(line, carry):
+            to_x, to_y = (x + line // 2) % 4, (y + line // 8) % 4
+            for other in (1, 0):
+                shard = shard_of(to_x, to_y, (my_low + other) % 2, (core + line) % 2)
+
+                @pl.when((shard != my_shard) | (tensor != my_tensor))
+                def _():
+                    pltpu.make_async_remote_copy(
+                        src_ref=upd.at[tensor, shard],
+                        dst_ref=out.at[y, my_low, x, core, my_tensor],
+                        send_sem=back_send_sem,
+                        recv_sem=back_recv_sem,
+                        device_id=(shard, tensor),
+                        device_id_type=MESH,
+                    ).start()
+            return carry
+
+        lax.fori_loop(0, 32, to_line, 0)
 
     def step_and_send(step, carry):
-        second_step(step, carry)
-        send_strip(step)
+        tensor = (my_tensor + 2 + step) % 4
+        second_step(tensor)
+        send_panel(tensor)
         return carry
 
     lax.fori_loop(0, 4, step_and_send, 0)
-    stay = pltpu.make_async_copy(piece(upd, my_shard, my_tensor), out.at[y, my_low, x, core, my_tensor], back_recv_sem)
+    stay = pltpu.make_async_copy(upd.at[my_tensor, my_shard], out.at[y, my_low, x, core, my_tensor], back_recv_sem)
     stay.start()
 
     sent = whole.at[pl.ds(0, 63)]
@@ -250,11 +233,10 @@
             pltpu.VMEM(by_column, jnp.bfloat16),
             pltpu.VMEM(by_owner, jnp.bfloat16),
             pltpu.VMEM(block, jnp.bfloat16),
-            pltpu.VMEM(square, jnp.float32),
             pltpu.VMEM(square, jnp.bfloat16),
             pltpu.VMEM(square, jnp.bfloat16),
             pltpu.VMEM(block, jnp.bfloat16),
-            pltpu.VMEM(block, jnp.bfloat16),
+            pltpu.VMEM((4, 64, 16, 256), jnp.bfloat16),
             pltpu.SemaphoreType.DMA((2, 16)),
             pltpu.SemaphoreType.REGULAR,
             pltpu.SemaphoreType.DMA,

time: 110 us -> 110 us (level)
  no operation moved by 1% of the time
where the time goes in v4:
time: 110 us; the launch traced here: 109 us
  Pallas kernels  109 us (99%)
    pallas_call x1, Pallas kernels, shards(): pl.pallas_call(kernel, name='muon', out_shape=(pltpu.VMEM(by_column, jnp....  106 us
    pallas_call x1, Pallas kernels, shards(): pl.pallas_call(write_out, name='write_out', out_shape=(jax.ShapeDtypeStru...  2.72 us

profile of v4, /device:TPU:1, one launch (start us, length us, event | category | flops | bytes accessed | tf_op | source)
XLA Modules:
  0.0 109.4 jit_solution(10180692593115626366)
XLA Ops:
  0.6 106.1 %muon.1 = (f32[4,2,4,8,16,256]{5,4,3,2,1,0:T(8,128)S(1)}, bf16[4,2,4,2,4,16,256]{6,5,4,3,2,1,0:T(8,128)(2,1)S(1)}) custom-call(bf16[4,2,4,8,16,256]{5,4,3,2,1,0:T(8,128)(2,1)} %bitcast.7, f32[4,2,4,8,16,256]{5,4,3,2,1,0:T(8,128)} %bitcast.6), custom_call_target="tpu_custom_call" | custom-call | tf_op jit(solution)/shard_map/muon/pallas_call | solution.py:226
  106.7 2.7 %write_out.1 = (f32[256,16,256]{2,1,0:T(8,128)}, bf16[256,16,256]{2,1,0:T(8,128)(2,1)}) custom-call(f32[256,16,256]{2,1,0:T(8,128)S(1)} %bitcast.4, bf16[256,16,256]{2,1,0:T(8,128)(2,1)S(1)} %bitcast.5), custom_call_target="tpu_custom_call" | custom-call | tf_op jit(solution)/shard_map/write_out/pallas_call | solution.py:249

commit v5 on v4

--- a/solution.py
+++ b/solution.py
@@ -11,6 +11,7 @@
 A, B, C = 3.4445, -4.775, 2.0315
 EARLY = 5
 HOPS = (4, 1, -1, 2, -2, 3, -3, 0)
+PARTS = 8
 OWNERS = (4, 2, 4, 2, 4)
 
 
@@ -55,12 +56,16 @@
             pl.semaphore_signal(barrier, inc=1, device_id=(shard_of(x, y, low, to_core), tensor), device_id_type=MESH)
 
     def greet(step, carry):
-        to_x, to_y = column(step)
-        for to_core in (0, 1):
-            pl.semaphore_signal(barrier, inc=1, device_id=(shard_of(to_x, to_y, my_low, to_core), my_tensor), device_id_type=MESH)
-        return carry
-
-    lax.fori_loop(1, 16, greet, 0)
+        to_x, to_y = (x + 2 + step % 4) % 4, (y + 2 + step // 4) % 4
+
+        @pl.when(step != 10)
+        def _():
+            for to_core in (0, 1):
+                pl.semaphore_signal(barrier, inc=1, device_id=(shard_of(to_x, to_y, my_low, to_core), my_tensor), device_id_type=MESH)
+
+        return carry
+
+    lax.fori_loop(0, 16, greet, 0)
     pl.semaphore_signal(barrier, inc=1, device_id=(shard_of(x, y, my_low, 1 - core), my_tensor), device_id_type=MESH)
     lax.fori_loop(2, 16, start_load, 0)
 
@@ -208,7 +213,11 @@
 
 
 def write_out(kept, out, kept_hbm, out_hbm, sem):
-    copies = [pltpu.make_async_copy(kept, kept_hbm, sem.at[0]), pltpu.make_async_copy(out, out_hbm, sem.at[1])]
+    copies = []
+    for i in range(PARTS):
+        part = pl.ds(i * (256 // PARTS), 256 // PARTS)
+        copies.append(pltpu.make_async_copy(kept.at[part], kept_hbm.at[part], sem.at[0, i]))
+        copies.append(pltpu.make_async_copy(out.at[part], out_hbm.at[part], sem.at[1, i]))
     for copy in copies:
         copy.start()
     for copy in copies:
@@ -255,7 +264,7 @@
         ),
         in_specs=[vmem, vmem],
         out_specs=(hbm, hbm),
-        scratch_shapes=[pltpu.SemaphoreType.DMA((2,))],
+        scratch_shapes=[pltpu.SemaphoreType.DMA((2, PARTS))],
         compiler_params=pltpu.CompilerParams(vmem_limit_bytes=2**20),
     )(kept.reshape(momentum.shape), update.reshape(grads.shape))
 

time: 110 us -> 109 us (level)
  no operation moved by 1% of the time
where the time goes in v5:
time: 109 us
  Pallas kernels  109 us (100%)
    pallas_call x1, Pallas kernels, shards(): pl.pallas_call(kernel, name='muon', out_shape=(pltpu.VMEM(by_column, jnp....  106 us
    pallas_call x1, Pallas kernels, shards(): pl.pallas_call(write_out, name='write_out', out_shape=(jax.ShapeDtypeStru...  2.78 us

profile of v5, /device:TPU:1, one launch (start us, length us, event | category | flops | bytes accessed | tf_op | source)
XLA Modules:
  0.0 109.2 jit_solution(13311636048695569280)
XLA Ops:
  0.6 105.8 %muon.1 = (f32[4,2,4,8,16,256]{5,4,3,2,1,0:T(8,128)S(1)}, bf16[4,2,4,2,4,16,256]{6,5,4,3,2,1,0:T(8,128)(2,1)S(1)}) custom-call(bf16[4,2,4,8,16,256]{5,4,3,2,1,0:T(8,128)(2,1)} %bitcast.7, f32[4,2,4,8,16,256]{5,4,3,2,1,0:T(8,128)} %bitcast.6), custom_call_target="tpu_custom_call" | custom-call | tf_op jit(solution)/shard_map/muon/pallas_call | solution.py:235
  106.4 2.8 %write_out.1 = (f32[256,16,256]{2,1,0:T(8,128)}, bf16[256,16,256]{2,1,0:T(8,128)(2,1)}) custom-call(f32[256,16,256]{2,1,0:T(8,128)S(1)} %bitcast.4, bf16[256,16,256]{2,1,0:T(8,128)(2,1)S(1)} %bitcast.5), custom_call_target="tpu_custom_call" | custom-call | tf_op jit(solution)/shard_map/write_out/pallas_call | solution.py:258

commit v6 on v5

--- a/solution.py
+++ b/solution.py
@@ -11,7 +11,6 @@
 A, B, C = 3.4445, -4.775, 2.0315
 EARLY = 5
 HOPS = (4, 1, -1, 2, -2, 3, -3, 0)
-PARTS = 8
 OWNERS = (4, 2, 4, 2, 4)
 
 
@@ -35,19 +34,16 @@
     def column(step):
         return (x + step % 4) % 4, (y + step // 4) % 4
 
-    def load(step):
-        to_x, to_y = column(step)
+    def load(plane):
+        to_y = (y + plane) % 4
         return (
-            pltpu.make_async_copy(grads.at[to_y, :, to_x], fresh.at[to_y, :, to_x], load_sem.at[0, step]),
-            pltpu.make_async_copy(momentum.at[to_y, :, to_x], kept.at[to_y, :, to_x], load_sem.at[1, step]),
+            pltpu.make_async_copy(grads.at[to_y], fresh.at[to_y], load_sem.at[0, plane]),
+            pltpu.make_async_copy(momentum.at[to_y], kept.at[to_y], load_sem.at[1, plane]),
         )
 
-    def start_load(step, carry):
-        for copy in load(step):
+    for plane in range(4):
+        for copy in load(plane):
             copy.start()
-        return carry
-
-    lax.fori_loop(0, 2, start_load, 0)
 
     barrier = pltpu.get_barrier_semaphore()
     for hop in (4, 3, -3, 2, -2, 1, -1):
@@ -67,11 +63,13 @@
 
     lax.fori_loop(0, 16, greet, 0)
     pl.semaphore_signal(barrier, inc=1, device_id=(shard_of(x, y, my_low, 1 - core), my_tensor), device_id_type=MESH)
-    lax.fori_loop(2, 16, start_load, 0)
 
     def blend(step, carry):
-        for copy in load(step):
-            copy.wait()
+        @pl.when(step % 4 == 0)
+        def _():
+            for copy in load(step // 4):
+                copy.wait()
+
         to_x, to_y = column(step)
         for low in (0, 1):
             grads_f = fresh[to_y, low, to_x].astype(jnp.float32)
@@ -213,11 +211,7 @@
 
 
 def write_out(kept, out, kept_hbm, out_hbm, sem):
-    copies = []
-    for i in range(PARTS):
-        part = pl.ds(i * (256 // PARTS), 256 // PARTS)
-        copies.append(pltpu.make_async_copy(kept.at[part], kept_hbm.at[part], sem.at[0, i]))
-        copies.append(pltpu.make_async_copy(out.at[part], out_hbm.at[part], sem.at[1, i]))
+    copies = [pltpu.make_async_copy(kept, kept_hbm, sem.at[0]), pltpu.make_async_copy(out, out_hbm, sem.at[1])]
     for copy in copies:
         copy.start()
     for copy in copies:
@@ -246,7 +240,7 @@
             pltpu.VMEM(square, jnp.bfloat16),
             pltpu.VMEM(block, jnp.bfloat16),
             pltpu.VMEM((4, 64, 16, 256), jnp.bfloat16),
-            pltpu.SemaphoreType.DMA((2, 16)),
+            pltpu.SemaphoreType.DMA((2, 4)),
             pltpu.SemaphoreType.REGULAR,
             pltpu.SemaphoreType.DMA,
             pltpu.SemaphoreType.DMA,
@@ -264,7 +258,7 @@
         ),
         in_specs=[vmem, vmem],
         out_specs=(hbm, hbm),
-        scratch_shapes=[pltpu.SemaphoreType.DMA((2, PARTS))],
+        scratch_shapes=[pltpu.SemaphoreType.DMA((2,))],
         compiler_params=pltpu.CompilerParams(vmem_limit_bytes=2**20),
     )(kept.reshape(momentum.shape), update.reshape(grads.shape))
 

time: 109 us -> 109 us (level)
  no operation moved by 1% of the time
where the time goes in v6:
time: 109 us
  Pallas kernels  108 us (99%)
    pallas_call x1, Pallas kernels, shards(): pl.pallas_call(kernel, name='muon', out_shape=(pltpu.VMEM(by_column, jnp....  106 us
    pallas_call x1, Pallas kernels, shards(): pl.pallas_call(write_out, name='write_out', out_shape=(jax.ShapeDtypeStru...  2.72 us

profile of v6, /device:TPU:1, one launch (start us, length us, event | category | flops | bytes accessed | tf_op | source)
XLA Modules:
  0.0 108.9 jit_solution(6566336768160264288)
XLA Ops:
  0.6 105.6 %muon.1 = (f32[4,2,4,8,16,256]{5,4,3,2,1,0:T(8,128)S(1)}, bf16[4,2,4,2,4,16,256]{6,5,4,3,2,1,0:T(8,128)(2,1)S(1)}) custom-call(bf16[4,2,4,8,16,256]{5,4,3,2,1,0:T(8,128)(2,1)} %bitcast.7, f32[4,2,4,8,16,256]{5,4,3,2,1,0:T(8,128)} %bitcast.6), custom_call_target="tpu_custom_call" | custom-call | tf_op jit(solution)/shard_map/muon/pallas_call | solution.py:229
  106.2 2.7 %write_out.1 = (f32[256,16,256]{2,1,0:T(8,128)}, bf16[256,16,256]{2,1,0:T(8,128)(2,1)}) custom-call(f32[256,16,256]{2,1,0:T(8,128)S(1)} %bitcast.4, bf16[256,16,256]{2,1,0:T(8,128)(2,1)S(1)} %bitcast.5), custom_call_target="tpu_custom_call" | custom-call | tf_op jit(solution)/shard_map/write_out/pallas_call | solution.py:252

commit v7 on v6

--- a/solution.py
+++ b/solution.py
@@ -93,7 +93,7 @@
             device_id_type=MESH,
         ).start()
 
-    lax.fori_loop(0, 2, blend, 0)
+    lax.fori_loop(0, 4, blend, 0)
     pl.semaphore_wait(barrier, 45)
     for hop in (4, 3, -3, 2, -2, 1, -1):
         low, tensor = depth(hop)
@@ -106,7 +106,7 @@
     forward(x, y, 0, 1 - core)
     own = pltpu.make_async_copy(nest.at[y, my_low, x, core, my_tensor], piece(whole, my_shard, my_tensor), recv_sem)
     own.start()
-    lax.fori_loop(2, EARLY + 1, blend, 0)
+    lax.fori_loop(4, EARLY + 1, blend, 0)
     pl.semaphore_wait(ready_sem, 7)
 
     def to_column(to_core, blending):

time: 109 us -> 109 us (level)
  no operation moved by 1% of the time
where the time goes in v7:
time: 109 us
  Pallas kernels  108 us (99%)
    pallas_call x1, Pallas kernels, shards(): pl.pallas_call(kernel, name='muon', out_shape=(pltpu.VMEM(by_column, jnp....  106 us
    pallas_call x1, Pallas kernels, shards(): pl.pallas_call(write_out, name='write_out', out_shape=(jax.ShapeDtypeStru...  2.72 us

profile of v7, /device:TPU:1, one launch (start us, length us, event | category | flops | bytes accessed | tf_op | source)
XLA Modules:
  0.0 108.9 jit_solution(11202429351178126716)
XLA Ops:
  0.6 105.6 %muon.1 = (f32[4,2,4,8,16,256]{5,4,3,2,1,0:T(8,128)S(1)}, bf16[4,2,4,2,4,16,256]{6,5,4,3,2,1,0:T(8,128)(2,1)S(1)}) custom-call(bf16[4,2,4,8,16,256]{5,4,3,2,1,0:T(8,128)(2,1)} %bitcast.7, f32[4,2,4,8,16,256]{5,4,3,2,1,0:T(8,128)} %bitcast.6), custom_call_target="tpu_custom_call" | custom-call | tf_op jit(solution)/shard_map/muon/pallas_call | solution.py:229
  106.2 2.7 %write_out.1 = (f32[256,16,256]{2,1,0:T(8,128)}, bf16[256,16,256]{2,1,0:T(8,128)(2,1)}) custom-call(f32[256,16,256]{2,1,0:T(8,128)S(1)} %bitcast.4, bf16[256,16,256]{2,1,0:T(8,128)(2,1)S(1)} %bitcast.5), custom_call_target="tpu_custom_call" | custom-call | tf_op jit(solution)/shard_map/write_out/pallas_call | solution.py:252
